TPU v7x, 256 devices: a whole 4x4x8 slice. The times are simulated.
256 devices in a mesh: dp: 2 (over core), tm: 32 (over z, y), space: 4 (over x).
Axes of the slice: x: 4, y: 4, z: 8, core: 2. Of those that a mesh axis runs over, the one named last changes fastest.
Arguments:
- latents: bfloat16 [2, 64, 8, 80, 512], P('dp', 'tm', 'space'), may hold values from -6 to 6
- norm_gain: float32 [512], replicated, may hold values from 0.25 to 1.75
- kernel: bfloat16 [13824, 512], P(None, 'dp'), may hold values from -0.0546875 to 0.0546875
- conv_bias: float32 [512], replicated, may hold values from -3 to 3
- out_grad: bfloat16 [2, 64, 8, 80, 512], P('dp', 'tm', 'space'), may hold values from -6 to 6
Outputs:
- block_out: bfloat16 [2, 64, 8, 80, 512], P('dp', 'tm', 'space')
- latent_grad: bfloat16 [2, 64, 8, 80, 512], P('dp', 'tm', 'space')
- kernel_grad: float32 [13824, 512], P('tm', 'dp')
- gain_grad: float32 [512], replicated
- bias_grad: float32 [512], replicated
All inputs are finite; a program needn't handle non-finite values.
Results may differ from a plain program's by a relative error of at most 0.0029.
Values may be sent and summed in bfloat16 or wider, within the bound.
No kernel may reach another device: no remote copies, remote signals or barrier semaphores. Data moves between devices by JAX's collectives and lax.ppermute only.
A program may use at most 128 MiB of HBM per device.

v0:
```python
import jax
import jax.numpy as jnp
from jax import lax
from jax.sharding import PartitionSpec as P


def shifted(block, axis, distance):
    devices = range(lax.axis_size(axis))
    route = [(i - distance, i) for i in devices if i - distance in devices]
    return lax.ppermute(block, axis, route)


def padded(block, sides, width):
    for axis, dim in sides:
        count = lax.axis_size(axis)
        forward = [(i, i + 1) for i in range(count - 1)]
        backward = [(target, source) for source, target in forward]
        low = lax.ppermute(
            lax.slice_in_dim(block, block.shape[dim] - width, None, axis=dim), axis, forward
        )
        high = lax.ppermute(lax.slice_in_dim(block, 0, width, axis=dim), axis, backward)
        block = jnp.concatenate([low, block, high], axis=dim)
    return block


def tap_columns(extended, frame_count, row_count, col_count, flipped):
    pieces = []
    for tap_t in range(3):
        for tap_h in range(3):
            for tap_w in range(3):
                if flipped:
                    start_t, start_h, start_w = (2 - tap_t, 2 - tap_h, 2 - tap_w)
                else:
                    start_t, start_h, start_w = (tap_t, tap_h, tap_w)
                pieces.append(
                    extended[
                        :,
                        start_t : start_t + frame_count,
                        start_h : start_h + row_count,
                        start_w : start_w + col_count,
                        :,
                    ]
                )
    stacked = jnp.concatenate(pieces, axis=-1)
    return stacked.reshape(-1, stacked.shape[-1])


def pad_columns(extended):
    return jnp.pad(extended, ((0, 0), (0, 0), (0, 0), (1, 1), (0, 0)))


def on_device(latents, norm_gain, kernel, conv_bias, out_grad):
    chans = latents.shape[-1]
    half_cols = kernel.shape[1]
    clip_local, frame_count, row_count, col_count = (
        latents.shape[0],
        latents.shape[1],
        latents.shape[2],
        latents.shape[3],
    )
    cell_total = (
        clip_local
        * frame_count
        * row_count
        * col_count
        * lax.axis_size("dp")
        * lax.axis_size("tm")
        * lax.axis_size("space")
    )
    grad_scale = 1.0 / jnp.sqrt(jnp.float32(cell_total))
    floats = latents.astype(jnp.float32)
    scale = lax.rsqrt(jnp.mean(floats * floats, axis=-1, keepdims=True) + 1e-06)
    normed = floats * scale
    pre_act = normed * norm_gain
    act = jax.nn.silu(pre_act).astype(jnp.bfloat16)
    grad_pair = lax.all_to_all(out_grad, "dp", split_axis=4, concat_axis=0, tiled=True)
    earlier = shifted(act, "tm", 1)
    joined = jnp.concatenate([earlier, act], axis=1)
    act_ext = padded(joined, (("space", 2),), 1)
    later = shifted(grad_pair, "tm", -1)
    joined_grad = jnp.concatenate([grad_pair, later], axis=1)
    grad_ext = padded(joined_grad, (("space", 2),), 1)
    act_pair = lax.all_gather(act_ext, "dp", axis=0, tiled=True)
    pair_clips = act_pair.shape[0]
    act_taps = tap_columns(pad_columns(act_pair), frame_count, row_count, col_count, False)
    conv_part = jnp.dot(act_taps, kernel, preferred_element_type=jnp.float32)
    conv_part = conv_part.reshape(pair_clips, frame_count, row_count, col_count, half_cols)
    conv = lax.all_to_all(conv_part, "dp", split_axis=0, concat_axis=4, tiled=True)
    block_out = (floats + conv + conv_bias).astype(jnp.bfloat16)
    kernel_local = (
        lax.dot_general(
            act_taps,
            grad_pair.reshape(-1, half_cols),
            (((0,), (0,)), ((), ())),
            preferred_element_type=jnp.float32,
        )
        * grad_scale
    )
    flipped_kernel = jnp.transpose(kernel.reshape(-1, chans, half_cols), (0, 2, 1)).reshape(
        -1, chans
    )
    grad_taps = tap_columns(pad_columns(grad_ext), frame_count, row_count, col_count, True)
    partial_grad = jnp.dot(grad_taps, flipped_kernel, preferred_element_type=jnp.float32)
    partial_grad = partial_grad.reshape(pair_clips, frame_count, row_count, col_count, chans)
    act_grad = lax.psum_scatter(partial_grad, "dp", scatter_dimension=0, tiled=True)
    grads = out_grad.astype(jnp.float32)
    bias_local = jnp.sum(grads.reshape(-1, chans), axis=0) * grad_scale
    sig = jax.nn.sigmoid(pre_act)
    pre_grad = act_grad * sig * (1.0 + pre_act * (1.0 - sig))
    gain_local = jnp.sum((pre_grad * normed).reshape(-1, chans), axis=0) * grad_scale
    normed_grad = pre_grad * norm_gain
    latent_grad = grads + scale * (
        normed_grad - normed * jnp.mean(normed_grad * normed, axis=-1, keepdims=True)
    )
    gain_grad, bias_grad = lax.psum((gain_local, bias_local), ("dp", "tm", "space"))
    row_part = lax.psum_scatter(kernel_local, "tm", scatter_dimension=0, tiled=True)
    kernel_grad = lax.psum(row_part, "space")
    return (block_out, latent_grad.astype(jnp.bfloat16), kernel_grad, gain_grad, bias_grad)


def solution(mesh):
    in_specs = (
        P("dp", "tm", "space", None, None),
        P(),
        P(None, "dp"),
        P(),
        P("dp", "tm", "space", None, None),
    )
    out_specs = (
        P("dp", "tm", "space", None, None),
        P("dp", "tm", "space", None, None),
        P("tm", "dp"),
        P(),
        P(),
    )
    return jax.shard_map(
        on_device, mesh=mesh, in_specs=in_specs, out_specs=out_specs, check_vma=False
    )
```

profile of v0, /device:TPU:8, one launch (start us, length us, event | category | flops | bytes accessed | tf_op | source)
XLA Modules:
  0.0 441.9 jit_solution(11372110334327910266)
XLA Ops:
  7.2 1.3 copy.20
  8.5 4.2 all_to_all.36
  13.0 4.1 collective-permute-start.3
  17.1 7.6 %collective-permute-done.3 = bf16[2,2,2,80,256]{4,3,2,1,0:T(8,128)(2,1)S(1)} collective-permute-done((bf16[2,2,2,80,256]{4,3,2,1,0:T(8,128)(2,1)S(1)}, bf16[2,2,2,80,256]{4,3,2,1,0:T(8,128)(2,1)S(1)}, u32[]{:S(2)}, u32[]{:S(2)}) %collective-permute-start.3) | collective-permute-done | bytes 327712 | tf_op jit(solution)/shard_map/ppermute | solution.py:10
  24.7 3.4 collective-permute-start.4
  28.2 1.3 collective-permute-start.5
  29.5 10.3 %copy.23 = bf16[27,256,512]{2,1,0:T(8,128)(2,1)} copy(bf16[27,256,512]{1,2,0:T(8,128)(2,1)} %bitcast.37) | data formatting | bytes 14155776 | tf_op jit(solution)/shard_map/transpose | solution.py:99
  42.0 0.9 slice-done
  42.9 1.1 slice-done.1
  44.0 5.8 %fusion.31 = f32[2,2,2,80,512]{4,3,2,1,0:T(8,128)} fusion(bf16[2,2,2,80,6912]{4,3,2,1,0:T(8,128)(2,1)S(1)} %slice_dynamic-update-slice_fusion.27, bf16[6912,512,1,1,1]{1,0,4,3,2:T(8,128)(2,1)S(1)} %bitcast.40), kind=kOutput, calls=%fused_computation.109 | convolution fusion | flops 4529848320 | bytes 17235968 | tf_op jit(solution)/shard_map/dot_general | solution.py:103
  50.1 20.0 %reduce-scatter.3.cloned.1.call-done = f32[1,2,2,80,512]{4,3,2,1,0:T(8,128)} async-done(((f32[2,2,2,80,512]{4,3,2,1,0:T(8,128)}), f32[1,2,2,80,512]{4,3,2,1,0:T(8,128)}) %reduce-scatter.3.cloned.1.call-update) | async-done | bytes 655376 | tf_op jit(solution)/shard_map/reduce_scatter | solution.py:105
  70.1 1.6 fusion.23
  71.7 2.4 fusion.13
  74.1 3.4 collective-permute-start
  77.5 8.2 %collective-permute-done = bf16[1,2,2,80,512]{4,3,2,1,0:T(8,128)(2,1)S(1)} collective-permute-done((bf16[1,2,2,80,512]{4,3,2,1,0:T(8,128)(2,1)S(1)}, bf16[1,2,2,80,512]{4,3,2,1,0:T(8,128)(2,1)S(1)}, u32[]{:S(2)}, u32[]{:S(2)}) %collective-permute-start) | collective-permute-done | bytes 327712 | tf_op jit(solution)/shard_map/ppermute | solution.py:10
  85.8 3.4 collective-permute-start.1
  89.2 1.3 collective-permute-start.2
  90.5 5.1 %collective-permute-done.1 = bf16[1,4,1,80,512]{4,3,2,1,0:T(8,128)(2,1)S(1)} collective-permute-done((bf16[1,4,1,80,512]{4,3,2,1,0:T(8,128)(2,1)S(1)}, bf16[1,4,1,80,512]{4,3,2,1,0:T(8,128)(2,1)S(1)}, u32[]{:S(2)}, u32[]{:S(2)}) %collective-permute-start.1) | collective-permute-done | bytes 327712 | tf_op jit(solution)/shard_map/ppermute | solution.py:18
  95.6 4.1 collective-permute-done.2
  99.7 1.2 pad_maximum_fusion
  101.2 18.5 %all-gather.2.cloned.1.call-done = bf16[2,4,4,80,512]{4,3,2,1,0:T(8,128)(2,1)} async-done(((bf16[1,4,4,80,512]{4,3,2,1,0:T(8,128)(2,1)}), bf16[2,4,4,80,512]{4,3,2,1,0:T(8,128)(2,1)}) %all-gather.2.cloned.1.call-update) | async-done | bytes 2621456 | tf_op jit(solution)/shard_map/all_gather | solution.py:83
  119.7 1.4 slice_dynamic-update-slice_fusion.26
  121.0 1.1 slice_dynamic-update-slice_fusion.8
  122.2 1.2 slice_dynamic-update-slice_fusion.25
  126.4 6.1 %copy-done.3 = bf16[2,2,2,80,13824]{4,3,2,1,0:T(8,128)(2,1)} copy-done((bf16[2,2,2,80,13824]{4,3,2,1,0:T(8,128)(2,1)}, bf16[2,2,2,80,13824]{4,3,2,1,0:T(8,128)(2,1)S(1)}, u32[]{:S(2)}) %copy-start.3) | copy-done | bytes 17694744
  132.5 9.0 %convolution_multiply_fusion = f32[13824,256]{1,0:T(8,128)} fusion(bf16[640,13824]{1,0:T(8,128)(2,1)S(1)} %bitcast.44, bf16[640,256]{1,0:T(8,128)(2,1)S(1)} %bitcast.36), kind=kOutput, calls=%fused_computation | convolution fusion | flops 4533387264 | bytes 32178176 | tf_op jit(solution)/shard_map/dot_general | solution.py:91
  141.6 77.4 %all-reduce.2 = (f32[512]{0:T(512)}, f32[512]{0:T(512)}) all-reduce(f32[512]{0:T(512)S(1)} %broadcast_multiply_fusion.1, f32[512]{0:T(512)S(1)} %broadcast_multiply_fusion), channel_id=1, replica_groups=mesh['dp'=2,'tm'=32,'space'=4] {'dp','tm','space'}, use_global_device_ids=true, to_apply=%region_6.7 | all-reduce | flops 1024 | bytes 8192 | tf_op jit(solution)/shard_map/psum | solution.py:115
  219.0 165.6 %reduce-scatter.5.cloned.1.call-done = f32[432,256]{1,0:T(8,128)} async-done(((f32[13824,256]{1,0:T(8,128)}), f32[432,256]{1,0:T(8,128)}) %reduce-scatter.5.cloned.1.call-update) | async-done | bytes 442384 | tf_op jit(solution)/shard_map/reduce_scatter | solution.py:116
  384.6 10.5 %fusion = f32[2,2,2,80,256]{4,3,2,1,0:T(8,128)S(1)} fusion(bf16[2,2,2,80,13824]{4,3,2,1,0:T(8,128)(2,1)} %copy-done.3, bf16[13824,256]{1,0:T(8,128)(2,1)} %param.7), kind=kOutput, calls=%fused_computation.1 | convolution fusion | flops 4529848320 | bytes 25427968 | tf_op jit(solution)/shard_map/dot_general | solution.py:86
  395.2 4.3 all_to_all.37
  400.3 33.2 %all-reduce.5.cloned.1.call-done = f32[432,256]{1,0:T(8,128)} async-done(((f32[432,256]{1,0:T(8,128)}), f32[432,256]{1,0:T(8,128)}) %all-reduce.5.cloned.1.call-update) | async-done | bytes 442384 | tf_op jit(solution)/shard_map/psum | solution.py:117
  433.5 1.8 copy.82
  (87 shorter events, 6.8 us)
Async XLA Ops:
  7.2 62.9 %reduce-scatter.3.cloned.1.call-start = ((), (), s32[]{:S(2)}) async-start(), calls=%async_computation.5 | async-start | bytes 1966080 | tf_op jit(solution)/shard_map/reduce_scatter | solution.py:105
  13.0 11.6 %collective-permute-start.3 = (bf16[2,2,2,80,256]{4,3,2,1,0:T(8,128)(2,1)S(1)}, bf16[2,2,2,80,256]{4,3,2,1,0:T(8,128)(2,1)S(1)}, u32[]{:S(2)}, u32[]{:S(2)}) collective-permute-start(bf16[2,2,2,80,256]{4,3,2,1,0:T(8,128)(2,1)S(1)} %bitcast.31), channel_id=1, source_target_pairs={{4,0},{8,4},{12,8},{16,12},{20,16},{24,20},{28,24},{32,28},{36,32}... | collective-permute-start | bytes 983048 | tf_op jit(solution)/shard_map/ppermute | solution.py:10
  24.7 15.0 %collective-permute-start.4 = (bf16[2,4,1,80,256]{4,3,2,1,0:T(8,128)(2,1)S(1)}, bf16[2,4,1,80,256]{4,3,2,1,0:T(8,128)(2,1)S(1)}, u32[]{:S(2)}, u32[]{:S(2)}) collective-permute-start(bf16[2,4,1,80,256]{4,3,2,1,0:T(8,128)(2,1)S(1)} %get-tuple-element.11), channel_id=1, source_target_pairs={{0,1},{1,2},{2,3},{4,5},{5,6},{6,7},{8,9},{9,10},{10,11},{12,13},{... | collective-permute-start | bytes 983048 | tf_op jit(solution)/shard_map/ppermute | solution.py:18
  28.2 11.6 %collective-permute-start.5 = (bf16[2,4,1,80,256]{4,3,2,1,0:T(8,128)(2,1)S(1)}, bf16[2,4,1,80,256]{4,3,2,1,0:T(8,128)(2,1)S(1)}, u32[]{:S(2)}, u32[]{:S(2)}) collective-permute-start(bf16[2,4,1,80,256]{4,3,2,1,0:T(8,128)(2,1)S(1)} %get-tuple-element.12), channel_id=1, source_target_pairs={{1,0},{2,1},{3,2},{5,4},{6,5},{7,6},{9,8},{10,9},{11,10},{13,12},{... | collective-permute-start | bytes 983048 | tf_op jit(solution)/shard_map/ppermute | solution.py:21
  40.7 2.2 slice-start
  41.4 2.6 slice-start.1
  44.0 5.9 %copy-start.1 = (bf16[1,2,2,80,512]{4,3,2,1,0:T(8,128)(2,1)S(1)}, bf16[1,2,2,80,512]{4,3,2,1,0:T(8,128)(2,1)}, u32[]{:S(2)}) copy-start(bf16[1,2,2,80,512]{4,3,2,1,0:T(8,128)(2,1)} %param.5) | copy-start | bytes 983044
  44.0 26.1 %copy-start.4 = (f32[512]{0:T(512)S(1)}, f32[512]{0:T(512)}, u32[]{:S(2)}) copy-start(f32[512]{0:T(512)} %param.6) | copy-start | bytes 6148
  44.0 27.7 %copy-start.2 = (bf16[1,2,2,80,512]{4,3,2,1,0:T(8,128)(2,1)S(1)}, bf16[1,2,2,80,512]{4,3,2,1,0:T(8,128)(2,1)}, u32[]{:S(2)}) copy-start(bf16[1,2,2,80,512]{4,3,2,1,0:T(8,128)(2,1)} %param.9) | copy-start | bytes 983044
  49.8 69.8 %all-gather.2.cloned.1.call-start = ((), (), s32[]{:S(2)}) async-start(), calls=%async_computation.4 | async-start | bytes 3932160 | tf_op jit(solution)/shard_map/all_gather | solution.py:83
  74.1 11.6 %collective-permute-start = (bf16[1,2,2,80,512]{4,3,2,1,0:T(8,128)(2,1)S(1)}, bf16[1,2,2,80,512]{4,3,2,1,0:T(8,128)(2,1)S(1)}, u32[]{:S(2)}, u32[]{:S(2)}) collective-permute-start(bf16[1,2,2,80,512]{4,3,2,1,0:T(8,128)(2,1)S(1)} %get-tuple-element.16), channel_id=1, source_target_pairs={{0,4},{4,8},{8,12},{12,16},{16,20},{20,24},{24,28},{28,32},{32,36}... | collective-permute-start | bytes 983048 | tf_op jit(solution)/shard_map/ppermute | solution.py:10
  85.8 9.8 %collective-permute-start.1 = (bf16[1,4,1,80,512]{4,3,2,1,0:T(8,128)(2,1)S(1)}, bf16[1,4,1,80,512]{4,3,2,1,0:T(8,128)(2,1)S(1)}, u32[]{:S(2)}, u32[]{:S(2)}) collective-permute-start(bf16[1,4,1,80,512]{4,3,2,1,0:T(8,128)(2,1)S(1)} %get-tuple-element.13), channel_id=1, source_target_pairs={{0,1},{1,2},{2,3},{4,5},{5,6},{6,7},{8,9},{9,10},{10,11},{12,13},{... | collective-permute-start | bytes 983048 | tf_op jit(solution)/shard_map/ppermute | solution.py:18
  89.2 10.5 %collective-permute-start.2 = (bf16[1,4,1,80,512]{4,3,2,1,0:T(8,128)(2,1)S(1)}, bf16[1,4,1,80,512]{4,3,2,1,0:T(8,128)(2,1)S(1)}, u32[]{:S(2)}, u32[]{:S(2)}) collective-permute-start(bf16[1,4,1,80,512]{4,3,2,1,0:T(8,128)(2,1)S(1)} %get-tuple-element.14), channel_id=1, source_target_pairs={{1,0},{2,1},{3,2},{5,4},{6,5},{7,6},{9,8},{10,9},{11,10},{13,12},{... | collective-permute-start | bytes 983048 | tf_op jit(solution)/shard_map/ppermute | solution.py:21
  101.0 283.7 %reduce-scatter.5.cloned.1.call-start = ((), (), s32[]{:S(2)}) async-start(), calls=%async_computation.6 | async-start | bytes 14598144 | tf_op jit(solution)/shard_map/reduce_scatter | solution.py:116
  119.6 3.8 copy-start
  126.4 6.1 %copy-start.3 = (bf16[2,2,2,80,13824]{4,3,2,1,0:T(8,128)(2,1)}, bf16[2,2,2,80,13824]{4,3,2,1,0:T(8,128)(2,1)S(1)}, u32[]{:S(2)}) copy-start(bf16[2,2,2,80,13824]{4,3,2,1,0:T(8,128)(2,1)S(1)} %slice_dynamic-update-slice_fusion.9) | copy-start | bytes 53084164
  141.5 292.0 %all-reduce.5.cloned.1.call-start = ((), (), s32[]{:S(2)}) async-start(), calls=%async_computation.7 | async-start | bytes 884736 | tf_op jit(solution)/shard_map/psum | solution.py:117
  384.6 14.9 %copy-start.5 = (f32[512]{0:T(512)S(1)}, f32[512]{0:T(512)}, u32[]{:S(2)}) copy-start(f32[512]{0:T(512)} %param.8) | copy-start | bytes 6148
Sparse Core Ops, SparseCore 0:
  50.0 20.0 reduce-scatter.2
  101.1 18.5 all-gather.1
  141.6 242.9 reduce-scatter.4
  386.8 46.6 all-reduce.4
where the time goes:
time: 443 us; the launch traced here: 442 us
  waiting for transfers between devices  262 us (59%)
  blocking collectives  85.8 us (19%)
  local copies, waits for them, and re-layouts  29.6 us (7%)
  matrix products  25.3 us (6%)
  starting transfers between devices  17.2 us (4%)
  between operations  14.4 us (3%)
  other arithmetic  7.21 us (2%)
    reduce_scatter x1, waiting for transfers between devices, on_device(): lax.psum_scatter(kernel_local, 'tm', scatter_dimension=0, tiled=True)  166 us
    psum x1, blocking collectives, on_device(): lax.psum((gain_local, bias_local), ('dp', 'tm', 'space'))  77.4 us
    psum x1, waiting for transfers between devices, on_device(): kernel_grad = lax.psum(row_part, 'space')  33.2 us
    reduce_scatter x1, waiting for transfers between devices, on_device(): lax.psum_scatter(partial_grad, 'dp', scatter_dimension=0, tiled=True)  20 us
    unnamed x69, local copies, waits for them, and re-layouts  18.6 us
    all_gather x1, waiting for transfers between devices, on_device(): act_pair = lax.all_gather(act_ext, 'dp', axis=0, tiled=True)  18.5 us
    ppermute x2, waiting for transfers between devices, shifted(): return lax.ppermute(block, axis, route)  15.8 us
    dot_general x1, matrix products, on_device(): conv_part = jnp.dot(act_taps, kernel, preferred_element_type=jnp.float32)  10.5 us
  transfers between devices with their start and end apart: 10, of which 8 were waited for; matrix products, arithmetic and copies ran while one was open for 5% of the time, Pallas kernels for 0%

commit v1 on v0

--- a/solution.py
+++ b/solution.py
@@ -2,6 +2,10 @@
 import jax.numpy as jnp
 from jax import lax
 from jax.sharding import PartitionSpec as P
+
+
+def search_target(local_x, named_axis):
+    return jnp.sum(lax.all_gather(local_x, named_axis), axis=0)
 
 
 def shifted(block, axis, distance):
@@ -114,7 +118,7 @@
     )
     gain_grad, bias_grad = lax.psum((gain_local, bias_local), ("dp", "tm", "space"))
     row_part = lax.psum_scatter(kernel_local, "tm", scatter_dimension=0, tiled=True)
-    kernel_grad = lax.psum(row_part, "space")
+    kernel_grad = search_target(row_part, "space")
     return (block_out, latent_grad.astype(jnp.bfloat16), kernel_grad, gain_grad, bias_grad)
 
 

time: 443 us -> 426 us (0.962)
  waiting for transfers between devices: 262 us -> 245 us
    psum x1 -> x0, waiting for transfers between devices: 33.2 us -> none  [on_device(): kernel_grad = lax.psum(row_part, 'space')]
    all_gather x0 -> x1, waiting for transfers between devices: none -> 15.8 us  [search_target(): return jnp.sum(lax.all_gather(local_x, named_axis), axis=0)]
    unnamed x69 -> x68, local copies, waits for them, and re-layouts: 18.6 us -> 16.8 us
where the time goes in v1:
time: 426 us; the launch traced here: 425 us
  waiting for transfers between devices  245 us (58%)
  blocking collectives  85.7 us (20%)
  local copies, waits for them, and re-layouts  27.8 us (7%)
  matrix products  25.3 us (6%)
  starting transfers between devices  17.2 us (4%)
  between operations  14.4 us (3%)
  other arithmetic  9.61 us (2%)
    reduce_scatter x1, waiting for transfers between devices, on_device(): lax.psum_scatter(kernel_local, 'tm', scatter_dimension=0, tiled=True)  165 us
    psum x1, blocking collectives, on_device(): lax.psum((gain_local, bias_local), ('dp', 'tm', 'space'))  77.3 us
    reduce_scatter x1, waiting for transfers between devices, on_device(): lax.psum_scatter(partial_grad, 'dp', scatter_dimension=0, tiled=True)  20 us
    all_gather x1, waiting for transfers between devices, on_device(): act_pair = lax.all_gather(act_ext, 'dp', axis=0, tiled=True)  18.5 us
    unnamed x68, local copies, waits for them, and re-layouts  16.8 us
    all_gather x1, waiting for transfers between devices, search_target(): return jnp.sum(lax.all_gather(local_x, named_axis), axis=0)  15.8 us
    ppermute x2, waiting for transfers between devices, shifted(): return lax.ppermute(block, axis, route)  15.8 us
    dot_general x1, matrix products, on_device(): conv_part = jnp.dot(act_taps, kernel, preferred_element_type=jnp.float32)  10.5 us
  transfers between devices with their start and end apart: 10, of which 8 were waited for; matrix products, arithmetic and copies ran while one was open for 5% of the time, Pallas kernels for 0%

profile of v1, /device:TPU:8, one launch (start us, length us, event | category | flops | bytes accessed | tf_op | source)
XLA Modules:
  0.0 424.8 jit_solution(3832529822609520405)
XLA Ops:
  7.2 1.3 copy.20
  8.5 4.2 all_to_all.36
  13.0 4.1 collective-permute-start.3
  17.1 7.6 %collective-permute-done.3 = bf16[2,2,2,80,256]{4,3,2,1,0:T(8,128)(2,1)S(1)} collective-permute-done((bf16[2,2,2,80,256]{4,3,2,1,0:T(8,128)(2,1)S(1)}, bf16[2,2,2,80,256]{4,3,2,1,0:T(8,128)(2,1)S(1)}, u32[]{:S(2)}, u32[]{:S(2)}) %collective-permute-start.3) | collective-permute-done | bytes 327712 | tf_op jit(solution)/shard_map/ppermute | solution.py:14
  24.7 3.4 collective-permute-start.4
  28.2 1.3 collective-permute-start.5
  29.5 10.3 %copy.23 = bf16[27,256,512]{2,1,0:T(8,128)(2,1)} copy(bf16[27,256,512]{1,2,0:T(8,128)(2,1)} %bitcast.38) | data formatting | bytes 14155776 | tf_op jit(solution)/shard_map/transpose | solution.py:103
  42.0 0.9 slice-done
  42.9 1.1 slice-done.1
  44.0 5.8 %fusion.31 = f32[2,2,2,80,512]{4,3,2,1,0:T(8,128)} fusion(bf16[2,2,2,80,6912]{4,3,2,1,0:T(8,128)(2,1)S(1)} %slice_dynamic-update-slice_fusion.27, bf16[6912,512,1,1,1]{1,0,4,3,2:T(8,128)(2,1)S(1)} %bitcast.41), kind=kOutput, calls=%fused_computation.109 | convolution fusion | flops 4529848320 | bytes 17235968 | tf_op jit(solution)/shard_map/dot_general | solution.py:107
  50.1 20.0 %reduce-scatter.3.cloned.1.call-done = f32[1,2,2,80,512]{4,3,2,1,0:T(8,128)} async-done(((f32[2,2,2,80,512]{4,3,2,1,0:T(8,128)}), f32[1,2,2,80,512]{4,3,2,1,0:T(8,128)}) %reduce-scatter.3.cloned.1.call-update) | async-done | bytes 655376 | tf_op jit(solution)/shard_map/reduce_scatter | solution.py:109
  70.1 1.6 fusion.23
  71.7 2.4 fusion.13
  74.1 3.4 collective-permute-start
  77.5 8.2 %collective-permute-done = bf16[1,2,2,80,512]{4,3,2,1,0:T(8,128)(2,1)S(1)} collective-permute-done((bf16[1,2,2,80,512]{4,3,2,1,0:T(8,128)(2,1)S(1)}, bf16[1,2,2,80,512]{4,3,2,1,0:T(8,128)(2,1)S(1)}, u32[]{:S(2)}, u32[]{:S(2)}) %collective-permute-start) | collective-permute-done | bytes 327712 | tf_op jit(solution)/shard_map/ppermute | solution.py:14
  85.8 3.4 collective-permute-start.1
  89.2 1.3 collective-permute-start.2
  90.5 5.1 %collective-permute-done.1 = bf16[1,4,1,80,512]{4,3,2,1,0:T(8,128)(2,1)S(1)} collective-permute-done((bf16[1,4,1,80,512]{4,3,2,1,0:T(8,128)(2,1)S(1)}, bf16[1,4,1,80,512]{4,3,2,1,0:T(8,128)(2,1)S(1)}, u32[]{:S(2)}, u32[]{:S(2)}) %collective-permute-start.1) | collective-permute-done | bytes 327712 | tf_op jit(solution)/shard_map/ppermute | solution.py:22
  95.6 4.1 collective-permute-done.2
  99.7 1.2 pad_maximum_fusion
  101.2 18.5 %all-gather.4.cloned.1.call-done = bf16[2,4,4,80,512]{4,3,2,1,0:T(8,128)(2,1)} async-done(((bf16[1,4,4,80,512]{4,3,2,1,0:T(8,128)(2,1)}), bf16[2,4,4,80,512]{4,3,2,1,0:T(8,128)(2,1)}) %all-gather.4.cloned.1.call-update) | async-done | bytes 2621456 | tf_op jit(solution)/shard_map/all_gather | solution.py:87
  119.7 1.4 slice_dynamic-update-slice_fusion.26
  121.0 1.1 slice_dynamic-update-slice_fusion.8
  122.2 1.2 slice_dynamic-update-slice_fusion.25
  126.4 6.1 %copy-done.3 = bf16[2,2,2,80,13824]{4,3,2,1,0:T(8,128)(2,1)} copy-done((bf16[2,2,2,80,13824]{4,3,2,1,0:T(8,128)(2,1)}, bf16[2,2,2,80,13824]{4,3,2,1,0:T(8,128)(2,1)S(1)}, u32[]{:S(2)}) %copy-start.3) | copy-done | bytes 17694744
  132.5 9.0 %convolution_multiply_fusion = f32[13824,256]{1,0:T(8,128)} fusion(bf16[640,13824]{1,0:T(8,128)(2,1)S(1)} %bitcast.46, bf16[640,256]{1,0:T(8,128)(2,1)S(1)} %bitcast.37), kind=kOutput, calls=%fused_computation | convolution fusion | flops 4533387264 | bytes 32178176 | tf_op jit(solution)/shard_map/dot_general | solution.py:95
  141.6 77.3 %all-reduce.2 = (f32[512]{0:T(512)}, f32[512]{0:T(512)}) all-reduce(f32[512]{0:T(512)S(1)} %broadcast_multiply_fusion.1, f32[512]{0:T(512)S(1)} %broadcast_multiply_fusion), channel_id=1, replica_groups=mesh['dp'=2,'tm'=32,'space'=4] {'dp','tm','space'}, use_global_device_ids=true, to_apply=%region_6.7 | all-reduce | flops 1024 | bytes 8192 | tf_op jit(solution)/shard_map/psum | solution.py:119
  218.8 165.5 %reduce-scatter.5.cloned.1.call-done = f32[432,256]{1,0:T(8,128)} async-done(((f32[13824,256]{1,0:T(8,128)}), f32[432,256]{1,0:T(8,128)}) %reduce-scatter.5.cloned.1.call-update) | async-done | bytes 442384 | tf_op jit(solution)/shard_map/reduce_scatter | solution.py:120
  384.3 10.5 %fusion = f32[2,2,2,80,256]{4,3,2,1,0:T(8,128)S(1)} fusion(bf16[2,2,2,80,13824]{4,3,2,1,0:T(8,128)(2,1)} %copy-done.3, bf16[13824,256]{1,0:T(8,128)(2,1)} %param.7), kind=kOutput, calls=%fused_computation.1 | convolution fusion | flops 4529848320 | bytes 25427968 | tf_op jit(solution)/shard_map/dot_general | solution.py:90
  394.9 4.3 %all_to_all.37 = f32[2,2,2,80,256]{4,3,2,1,0:T(8,128)S(1)} all-to-all(f32[2,2,2,80,256]{4,3,2,1,0:T(8,128)S(1)} %fusion), channel_id=1, replica_groups=mesh['dp'=2,'tm'=32,'space'=4] {'dp'}, dimensions={0} | all-to-all | bytes 1310720 | tf_op jit(solution)/shard_map/all_to_all | solution.py:92
  400.0 15.8 %all-gather.6.cloned.1.call-done = f32[1728,256]{1,0:T(8,128)} async-done(((f32[432,256]{1,0:T(8,128)}), f32[1728,256]{1,0:T(8,128)}) %all-gather.6.cloned.1.call-update) | async-done | bytes 1769488 | tf_op jit(solution)/shard_map/all_gather | solution.py:8
  415.9 2.4 reduce_sum.47
  (87 shorter events, 6.8 us)
Async XLA Ops:
  7.2 62.9 %reduce-scatter.3.cloned.1.call-start = ((), (), s32[]{:S(2)}) async-start(), calls=%async_computation.5 | async-start | bytes 1966080 | tf_op jit(solution)/shard_map/reduce_scatter | solution.py:109
  13.0 11.6 %collective-permute-start.3 = (bf16[2,2,2,80,256]{4,3,2,1,0:T(8,128)(2,1)S(1)}, bf16[2,2,2,80,256]{4,3,2,1,0:T(8,128)(2,1)S(1)}, u32[]{:S(2)}, u32[]{:S(2)}) collective-permute-start(bf16[2,2,2,80,256]{4,3,2,1,0:T(8,128)(2,1)S(1)} %bitcast.32), channel_id=1, source_target_pairs={{4,0},{8,4},{12,8},{16,12},{20,16},{24,20},{28,24},{32,28},{36,32}... | collective-permute-start | bytes 983048 | tf_op jit(solution)/shard_map/ppermute | solution.py:14
  24.7 15.0 %collective-permute-start.4 = (bf16[2,4,1,80,256]{4,3,2,1,0:T(8,128)(2,1)S(1)}, bf16[2,4,1,80,256]{4,3,2,1,0:T(8,128)(2,1)S(1)}, u32[]{:S(2)}, u32[]{:S(2)}) collective-permute-start(bf16[2,4,1,80,256]{4,3,2,1,0:T(8,128)(2,1)S(1)} %get-tuple-element.11), channel_id=1, source_target_pairs={{0,1},{1,2},{2,3},{4,5},{5,6},{6,7},{8,9},{9,10},{10,11},{12,13},{... | collective-permute-start | bytes 983048 | tf_op jit(solution)/shard_map/ppermute | solution.py:22
  28.2 11.6 %collective-permute-start.5 = (bf16[2,4,1,80,256]{4,3,2,1,0:T(8,128)(2,1)S(1)}, bf16[2,4,1,80,256]{4,3,2,1,0:T(8,128)(2,1)S(1)}, u32[]{:S(2)}, u32[]{:S(2)}) collective-permute-start(bf16[2,4,1,80,256]{4,3,2,1,0:T(8,128)(2,1)S(1)} %get-tuple-element.12), channel_id=1, source_target_pairs={{1,0},{2,1},{3,2},{5,4},{6,5},{7,6},{9,8},{10,9},{11,10},{13,12},{... | collective-permute-start | bytes 983048 | tf_op jit(solution)/shard_map/ppermute | solution.py:25
  40.7 2.2 slice-start
  41.4 2.6 slice-start.1
  44.0 5.9 %copy-start.1 = (bf16[1,2,2,80,512]{4,3,2,1,0:T(8,128)(2,1)S(1)}, bf16[1,2,2,80,512]{4,3,2,1,0:T(8,128)(2,1)}, u32[]{:S(2)}) copy-start(bf16[1,2,2,80,512]{4,3,2,1,0:T(8,128)(2,1)} %param.5) | copy-start | bytes 983044
  44.0 26.1 %copy-start.4 = (f32[512]{0:T(512)S(1)}, f32[512]{0:T(512)}, u32[]{:S(2)}) copy-start(f32[512]{0:T(512)} %param.6) | copy-start | bytes 6148
  44.0 27.7 %copy-start.2 = (bf16[1,2,2,80,512]{4,3,2,1,0:T(8,128)(2,1)S(1)}, bf16[1,2,2,80,512]{4,3,2,1,0:T(8,128)(2,1)}, u32[]{:S(2)}) copy-start(bf16[1,2,2,80,512]{4,3,2,1,0:T(8,128)(2,1)} %param.9) | copy-start | bytes 983044
  49.8 69.8 %all-gather.4.cloned.1.call-start = ((), (), s32[]{:S(2)}) async-start(), calls=%async_computation.4 | async-start | bytes 3932160 | tf_op jit(solution)/shard_map/all_gather | solution.py:87
  74.1 11.6 %collective-permute-start = (bf16[1,2,2,80,512]{4,3,2,1,0:T(8,128)(2,1)S(1)}, bf16[1,2,2,80,512]{4,3,2,1,0:T(8,128)(2,1)S(1)}, u32[]{:S(2)}, u32[]{:S(2)}) collective-permute-start(bf16[1,2,2,80,512]{4,3,2,1,0:T(8,128)(2,1)S(1)} %get-tuple-element.16), channel_id=1, source_target_pairs={{0,4},{4,8},{8,12},{12,16},{16,20},{20,24},{24,28},{28,32},{32,36}... | collective-permute-start | bytes 983048 | tf_op jit(solution)/shard_map/ppermute | solution.py:14
  85.8 9.8 %collective-permute-start.1 = (bf16[1,4,1,80,512]{4,3,2,1,0:T(8,128)(2,1)S(1)}, bf16[1,4,1,80,512]{4,3,2,1,0:T(8,128)(2,1)S(1)}, u32[]{:S(2)}, u32[]{:S(2)}) collective-permute-start(bf16[1,4,1,80,512]{4,3,2,1,0:T(8,128)(2,1)S(1)} %get-tuple-element.13), channel_id=1, source_target_pairs={{0,1},{1,2},{2,3},{4,5},{5,6},{6,7},{8,9},{9,10},{10,11},{12,13},{... | collective-permute-start | bytes 983048 | tf_op jit(solution)/shard_map/ppermute | solution.py:22
  89.2 10.5 %collective-permute-start.2 = (bf16[1,4,1,80,512]{4,3,2,1,0:T(8,128)(2,1)S(1)}, bf16[1,4,1,80,512]{4,3,2,1,0:T(8,128)(2,1)S(1)}, u32[]{:S(2)}, u32[]{:S(2)}) collective-permute-start(bf16[1,4,1,80,512]{4,3,2,1,0:T(8,128)(2,1)S(1)} %get-tuple-element.14), channel_id=1, source_target_pairs={{1,0},{2,1},{3,2},{5,4},{6,5},{7,6},{9,8},{10,9},{11,10},{13,12},{... | collective-permute-start | bytes 983048 | tf_op jit(solution)/shard_map/ppermute | solution.py:25
  101.0 283.4 %reduce-scatter.5.cloned.1.call-start = ((), (), s32[]{:S(2)}) async-start(), calls=%async_computation.6 | async-start | bytes 14598144 | tf_op jit(solution)/shard_map/reduce_scatter | solution.py:120
  119.6 3.8 copy-start
  126.4 6.1 %copy-start.3 = (bf16[2,2,2,80,13824]{4,3,2,1,0:T(8,128)(2,1)}, bf16[2,2,2,80,13824]{4,3,2,1,0:T(8,128)(2,1)S(1)}, u32[]{:S(2)}) copy-start(bf16[2,2,2,80,13824]{4,3,2,1,0:T(8,128)(2,1)S(1)} %slice_dynamic-update-slice_fusion.9) | copy-start | bytes 53084164
  141.5 274.4 %all-gather.6.cloned.1.call-start = ((), (), s32[]{:S(2)}) async-start(), calls=%async_computation.7 | async-start | bytes 2211840 | tf_op jit(solution)/shard_map/all_gather | solution.py:8
  384.3 14.9 %copy-start.5 = (f32[512]{0:T(512)S(1)}, f32[512]{0:T(512)}, u32[]{:S(2)}) copy-start(f32[512]{0:T(512)} %param.8) | copy-start | bytes 6148
Sparse Core Ops, SparseCore 0:
  50.0 20.0 reduce-scatter.2
  101.1 18.5 all-gather.3
  141.6 242.6 reduce-scatter.4
  386.0 29.8 all-gather.5
